TPU v7x, 32 devices: a whole 2x2x4 slice. The times are simulated.
32 devices in a mesh: groups: 2 (over y), slab: 4 (over z), batch: 2 (over x), chan: 2 (over core).
Axes of the slice: x: 2, y: 2, z: 4, core: 2. Of those that a mesh axis runs over, the one named last changes fastest.
Arguments:
- volume: bfloat16 [16, 8, 4, 8, 128], P(('groups', 'batch'), 'slab'), parts along dimension 0, may hold values from -6 to 6
- targets: float32 [16, 4], P(('groups', 'batch')), parts along dimension 0, may hold values from -1 to 1
- front_weight: bfloat16 [3, 3, 3, 128, 128], P(None, None, None, None, 'chan'), may hold values from -0.109375 to 0.109375
- stride_weight: bfloat16 [3, 3, 3, 128, 256], P(None, None, None, 'chan'), may hold values from -0.109375 to 0.109375
- hidden_weight: float32 [256, 128], P('chan'), may hold values from -0.375 to 0.375
- output_weight: float32 [128, 4], replicated, may hold values from -0.5 to 0.5
Outputs:
- grad_front: float32 [6, 3, 3, 128, 128], P('groups', None, None, None, 'chan'), parts along dimension 0
- grad_stride: float32 [6, 3, 3, 128, 256], P('groups', None, None, 'chan'), parts along dimension 0
- grad_hidden: float32 [512, 128], P(('groups', 'chan')), parts along dimension 0
- grad_output: float32 [256, 4], P('groups'), parts along dimension 0
- loss: float32 [2], P('groups'), parts along dimension 0
There are 2 independent parts, one for each index of `groups`. A program takes and returns all parts, laid end to end along the dimension named above; an argument that names none is the same for every part. Nothing has to cross between parts.
All inputs are finite; a program needn't handle non-finite values.
Results may differ from a plain program's by a relative error of at most 0.0052.
Values may be sent and summed in bfloat16 or wider, within the bound.
A program may use at most 64 MiB of HBM per device.

v0:
```python
import jax
import jax.numpy as jnp
from jax import lax
from jax.sharding import PartitionSpec as P


def with_halo(cells, sides, width):
    for axis, dim in sides:
        count = lax.axis_size(axis)
        ends = count - 1
        head = lax.slice_in_dim(cells, 0, width, axis=dim)
        tail = lax.slice_in_dim(cells, cells.shape[dim] - width, cells.shape[dim], axis=dim)
        cells = jnp.concatenate(
            [
                lax.ppermute(tail, axis, [(i, (i + 1) % count) for i in range(ends)]),
                cells,
                lax.ppermute(head, axis, [((i + 1) % count, i) for i in range(ends)]),
            ],
            axis=dim,
        )
    return cells


def swish_slope(preact):
    logistic = jax.nn.sigmoid(preact)
    return logistic * (1.0 + preact * (1.0 - logistic))


def tap_window(padded, tap_z, tap_x, tap_y, extent_z, extent_x, extent_y, stride):
    if stride == 1:
        return padded[
            :, tap_z : tap_z + extent_z, tap_x : tap_x + extent_x, tap_y : tap_y + extent_y, :
        ]
    leading = padded.shape[0]
    channels = padded.shape[-1]
    folded = padded.reshape(leading, extent_z + 1, 2, extent_x + 1, 2, extent_y + 1, 2, channels)
    return folded[
        :,
        tap_z // 2 : tap_z // 2 + extent_z,
        tap_z % 2,
        tap_x // 2 : tap_x // 2 + extent_x,
        tap_x % 2,
        tap_y // 2 : tap_y // 2 + extent_y,
        tap_y % 2,
        :,
    ]


def conv_apply(padded, weight, extent_z, extent_x, extent_y, stride):
    summed = None
    for tap_z in range(3):
        for tap_x in range(3):
            for tap_y in range(3):
                window = tap_window(
                    padded, tap_z, tap_x, tap_y, extent_z, extent_x, extent_y, stride
                )
                flat_tap = window.reshape(-1, window.shape[-1])
                contrib = jnp.dot(
                    flat_tap, weight[tap_z, tap_x, tap_y], preferred_element_type=jnp.float32
                )
                summed = contrib if summed is None else summed + contrib
    return summed.reshape(padded.shape[0], extent_z, extent_x, extent_y, weight.shape[-1])


def kernel_grad(padded, grad_out, extent_z, extent_x, extent_y, stride):
    flat_grad = grad_out.reshape(-1, grad_out.shape[-1])
    results = []
    for tap_z in range(3):
        for tap_x in range(3):
            for tap_y in range(3):
                window = tap_window(
                    padded, tap_z, tap_x, tap_y, extent_z, extent_x, extent_y, stride
                )
                flat_tap = window.reshape(-1, window.shape[-1])
                results.append(
                    lax.dot_general(
                        flat_tap,
                        flat_grad,
                        (((0,), (0,)), ((), ())),
                        preferred_element_type=jnp.float32,
                    )
                )
    return jnp.stack(results).reshape(3, 3, 3, padded.shape[-1], grad_out.shape[-1])


def input_grad(grad_out, weight, extent_z, extent_x, extent_y):
    leading = grad_out.shape[0]
    channels = weight.shape[3]
    flat_grad = grad_out.reshape(-1, grad_out.shape[-1])
    buckets = {}
    for tap_z in range(3):
        for tap_x in range(3):
            for tap_y in range(3):
                contrib = lax.dot_general(
                    flat_grad,
                    weight[tap_z, tap_x, tap_y],
                    (((1,), (1,)), ((), ())),
                    preferred_element_type=jnp.float32,
                )
                contrib = contrib.reshape(leading, extent_z, extent_x, extent_y, channels)
                placed = jnp.pad(
                    contrib,
                    (
                        (0, 0),
                        (tap_z // 2, 1 - tap_z // 2),
                        (tap_x // 2, 1 - tap_x // 2),
                        (tap_y // 2, 1 - tap_y // 2),
                        (0, 0),
                    ),
                )
                parity = (tap_z % 2, tap_x % 2, tap_y % 2)
                buckets[parity] = placed if parity not in buckets else buckets[parity] + placed
    planes_z = []
    for par_z in range(2):
        planes_x = []
        for par_x in range(2):
            planes_x.append(jnp.stack([buckets[par_z, par_x, par_y] for par_y in range(2)], axis=4))
        planes_z.append(jnp.stack(planes_x, axis=3))
    assembled = jnp.stack(planes_z, axis=2)
    assembled = assembled.reshape(
        leading, 2 * extent_z + 2, 2 * extent_x + 2, 2 * extent_y + 2, channels
    )
    return assembled[:, 1:-1, 1:-1, 1:-1, :]


def body(volume, targets, front_weight, stride_weight, hidden_weight, output_weight):
    highest = lax.Precision.HIGHEST
    slabs = lax.axis_size("slab")
    batches = lax.axis_size("batch")
    inner = front_weight.shape[-1]
    leading, thick, extent_x, extent_y, channels = volume.shape
    depth = thick * slabs
    outputs = output_weight.shape[-1]
    haloed = with_halo(volume, (("slab", 1),), 1)
    padded = jnp.pad(haloed, ((0, 0), (0, 0), (1, 1), (1, 1), (0, 0)))
    front_pre = conv_apply(padded, front_weight, thick, extent_x, extent_y, 1)
    front_act = jax.nn.silu(front_pre).astype(jnp.bfloat16)
    merged = front_act.reshape(leading, thick, extent_x, extent_y * inner)
    sample_act = lax.all_to_all(merged, "slab", split_axis=0, concat_axis=1, tiled=True)
    sample_act = sample_act.reshape(1, depth, extent_x, extent_y, inner)
    half_z = depth // 2
    half_x = extent_x // 2
    half_y = extent_y // 2
    cells = half_z * half_x * half_y
    stride_pad = jnp.pad(sample_act, ((0, 0), (1, 1), (1, 1), (1, 1), (0, 0)))
    partial_pre = conv_apply(stride_pad, stride_weight, half_z, half_x, half_y, 2)
    stride_pre = lax.psum_scatter(partial_pre, "chan", scatter_dimension=4, tiled=True)
    pooled = jnp.sum(jax.nn.silu(stride_pre), axis=(0, 1, 2, 3)) / cells
    hidden_pre = lax.psum(jnp.dot(pooled, hidden_weight, precision=highest), "chan")
    hidden_act = jax.nn.silu(hidden_pre)
    predicted = jnp.dot(hidden_act, output_weight, precision=highest)
    target_row = lax.dynamic_index_in_dim(targets, lax.axis_index("slab"), 0, keepdims=False)
    residual = predicted - target_row
    squared = jnp.sum(residual * residual)
    grad_output = jnp.outer(hidden_act, residual)
    grad_hidden_pre = jnp.dot(output_weight, residual, precision=highest) * swish_slope(hidden_pre)
    grad_hidden = jnp.outer(pooled, grad_hidden_pre)
    grad_pooled = jnp.dot(hidden_weight, grad_hidden_pre, precision=highest)
    grad_stride_pre = (grad_pooled / cells * swish_slope(stride_pre)).astype(jnp.bfloat16)
    full_grad = lax.all_gather(grad_stride_pre, "chan", axis=4, tiled=True)
    grad_stride = kernel_grad(stride_pad, full_grad, half_z, half_x, half_y, 2)
    grad_act = input_grad(full_grad, stride_weight, half_z, half_x, half_y).astype(jnp.bfloat16)
    returned = lax.all_to_all(
        grad_act.reshape(1, depth, extent_x, extent_y * inner),
        "slab",
        split_axis=1,
        concat_axis=0,
        tiled=True,
    )
    returned = returned.reshape(leading, thick, extent_x, extent_y, inner)
    grad_front_pre = (returned * swish_slope(front_pre)).astype(jnp.bfloat16)
    grad_front = kernel_grad(padded, grad_front_pre, thick, extent_x, extent_y, 1)
    grad_front, grad_stride, grad_hidden, grad_output, squared = lax.psum(
        (grad_front, grad_stride, grad_hidden, grad_output, squared), ("slab", "batch")
    )
    loss = (squared / (slabs * batches * outputs)).reshape(1)
    return (grad_front, grad_stride, grad_hidden, grad_output, loss)


def solution(mesh):
    in_specs = (
        P(("groups", "batch"), "slab", None, None, None),
        P(("groups", "batch"), None),
        P(None, None, None, None, "chan"),
        P(None, None, None, "chan", None),
        P("chan", None),
        P(),
    )
    out_specs = (
        P("groups", None, None, None, "chan"),
        P("groups", None, None, "chan", None),
        P(("groups", "chan"), None),
        P("groups", None),
        P("groups"),
    )
    return jax.shard_map(body, mesh=mesh, in_specs=in_specs, out_specs=out_specs, check_vma=False)
```

profile of v0, /device:TPU:0, one launch (start us, length us, event | category | flops | bytes accessed | tf_op | source)
XLA Modules:
  0.0 213.3 jit_solution(12655027647742667064)
XLA Ops:
  7.2 0.8 fusion.298
  8.0 4.9 %collective-permute-start = (bf16[4,1,4,8,128]{4,3,2,1,0:T(8,128)(2,1)S(1)}, bf16[4,1,4,8,128]{4,3,2,1,0:T(8,128)(2,1)S(1)}, u32[]{:S(2)}, u32[]{:S(2)}) collective-permute-start(bf16[4,1,4,8,128]{4,3,2,1,0:T(8,128)(2,1)S(1)} %get-tuple-element.63), channel_id=1, source_target_pairs={{0,4},{4,8},{8,12},{1,5},{5,9},{9,13},{2,6},{6,10},{10,14},{3,7},{... | collective-permute-start | bytes 98312 | tf_op jit(solution)/shard_map/ppermute | solution.py:15
  13.0 1.4 collective-permute-start.1
  14.5 4.4 %collective-permute-done.1 = bf16[4,1,4,8,128]{4,3,2,1,0:T(8,128)(2,1)S(1)} collective-permute-done((bf16[4,1,4,8,128]{4,3,2,1,0:T(8,128)(2,1)S(1)}, bf16[4,1,4,8,128]{4,3,2,1,0:T(8,128)(2,1)S(1)}, u32[]{:S(2)}, u32[]{:S(2)}) %collective-permute-start.1) | collective-permute-done | bytes 32800 | tf_op jit(solution)/shard_map/ppermute | solution.py:17
  18.9 1.0 select_maximum_fusion
  19.9 0.2 fusion.294
  20.2 0.6 copy-done.6
  25.4 9.3 %all_to_all.8 = bf16[4,2,4,512]{3,2,1,0:T(4,128)(2,1)S(1)} all-to-all(bf16[4,2,4,512]{3,2,1,0:T(4,128)(2,1)S(1)} %fusion.65), channel_id=1, replica_groups=mesh['groups'=2,'slab'=4,'batch'=2,'chan'=2] {'slab'}, dimensions={0} | all-to-all | bytes 65536 | tf_op jit(solution)/shard_map/all_to_all | solution.py:139
  35.1 0.2 fusion.296
  39.2 0.8 copy.165
  40.0 1.9 reshape.469
  41.9 6.1 %reduce-scatter.4.cloned.1.call-done = f32[128,32]{1,0:T(8,128)} async-done(((f32[256,32]{1,0:T(8,128)}), f32[128,32]{1,0:T(8,128)}) %reduce-scatter.4.cloned.1.call-update) | async-done | bytes 16400
  48.0 1.5 reshape.470
  49.5 0.4 copy.166
  50.1 2.5 %psum.42 = f32[128]{0:T(128)S(1)} all-reduce(f32[128]{0:T(128)S(1)} %convolution_bitcast_fusion.83), channel_id=1, replica_groups=mesh['groups'=2,'slab'=4,'batch'=2,'chan'=2] {'chan'}, use_global_device_ids=true, to_apply=%region_2.3 | all-reduce | flops 128 | bytes 1024 | tf_op jit(solution)/shard_map/psum | solution.py:149
  52.6 1.4 multiply_reduce_fusion.1
  54.4 1.8 all_gather.3
  65.4 0.7 reshape.468
  66.1 4.8 %all-to-all-start.1 = ((bf16[1,8,4,512]{3,2,0,1:T(4,128)(2,1)}), bf16[1,8,4,512]{3,2,0,1:T(4,128)(2,1)S(1)}, u32[]{:S(2)}, u32[]{:S(2)}) async-start(bf16[1,8,4,512]{3,2,0,1:T(4,128)(2,1)} %reshape.468), calls=%async_computation.1 | async-start | bytes 65536 | tf_op jit(solution)/shard_map/all_to_all | solution.py:163
  71.0 0.7 broadcast_multiply_fusion
  71.7 4.9 %all-to-all-done.1 = bf16[1,8,4,512]{3,2,0,1:T(4,128)(2,1)S(1)} async-done(((bf16[1,8,4,512]{3,2,0,1:T(4,128)(2,1)}), bf16[1,8,4,512]{3,2,0,1:T(4,128)(2,1)S(1)}, u32[]{:S(2)}, u32[]{:S(2)}) %all-to-all-start.1) | async-done | bytes 32800 | tf_op jit(solution)/shard_map/all_to_all | solution.py:163
  76.8 0.2 fusion.54
  77.0 0.2 fusion.53
  77.2 0.2 fusion.52
  77.4 0.2 fusion.51
  77.8 0.2 fusion.50
  78.0 0.2 fusion.49
  78.2 0.2 fusion.48
  78.5 0.2 fusion.47
  78.7 0.2 fusion.46
  78.9 0.2 fusion.45
  79.1 0.2 fusion.44
  79.3 0.2 fusion.43
  79.5 0.2 fusion.42
  79.7 0.2 fusion.41
  79.9 0.2 fusion.40
  80.5 0.2 fusion.37
  81.1 0.2 fusion.34
  81.5 0.2 fusion.33
  81.7 0.2 fusion.32
  81.9 0.2 fusion.31
  82.1 0.2 fusion.30
  82.4 0.9 copy-done.5
  83.4 20.3 %all-reduce.29 = (f32[128,4]{0,1:T(4,128)}, f32[]{:T(128)}) all-reduce(f32[128,4]{0,1:T(4,128)S(1)} %broadcast_multiply_fusion.1, f32[]{:T(128)} %get-tuple-element.65), channel_id=1, replica_groups=mesh['groups'=2,'slab'=4,'batch'=2,'chan'=2] {'slab','batch'}, use_global_device_ids=true, to_apply=%region_6.7 | all-reduce | flops 513 | bytes 4104 | tf_op jit(solution)/shard_map/psum | solution.py:173
  104.3 96.9 %all-reduce.33.cloned.1.call-done = (f32[3,3,3,128,64]{3,4,2,1,0:T(8,128)}, f32[3,3,3,64,256]{4,3,2,1,0:T(8,128)}, f32[128,128]{1,0:T(8,128)}) async-done(((f32[3,3,3,128,64]{3,4,2,1,0:T(8,128)}, f32[3,3,3,64,256]{4,3,2,1,0:T(8,128)}, f32[128,128]{1,0:T(8,128)}), (f32[3,3,3,128,64]{3,4,2,1,0:T(8,128)}, f32[3,3,3,64,256]{4,3,2,1,0:T(8,128)}, f32[128,128]{1,0:T(8,128)})) %all-reduce.33.cloned.1.call-update) | async-done | bytes 2719760 | tf_op jit(solution)/shard_map/psum | solution.py:173
  201.2 2.3 %copy.225 = f32[3,3,3,128,64]{3,4,2,1,0:T(8,128)} copy(f32[3,3,3,128,64]{3,4,2,1,0:T(8,128)} %get-tuple-element.73) | data formatting | bytes 1769472
  203.5 1.2 copy.226
  204.7 0.6 copy.227
  (204 shorter events, 19.8 us)
Async XLA Ops:
  7.2 42.8 %copy-start = (f32[128,128]{1,0:T(8,128)S(1)}, f32[128,128]{1,0:T(8,128)}, u32[]{:S(2)}) copy-start(f32[128,128]{1,0:T(8,128)} %param.10) | copy-start | bytes 196612
  7.2 40.8 %reduce-scatter.4.cloned.1.call-start = ((), (), s32[]{:S(2)}) async-start(), calls=%async_computation.3 | async-start | bytes 196608
  8.0 6.5 %collective-permute-start = (bf16[4,1,4,8,128]{4,3,2,1,0:T(8,128)(2,1)S(1)}, bf16[4,1,4,8,128]{4,3,2,1,0:T(8,128)(2,1)S(1)}, u32[]{:S(2)}, u32[]{:S(2)}) collective-permute-start(bf16[4,1,4,8,128]{4,3,2,1,0:T(8,128)(2,1)S(1)} %get-tuple-element.63), channel_id=1, source_target_pairs={{0,4},{4,8},{8,12},{1,5},{5,9},{9,13},{2,6},{6,10},{10,14},{3,7},{... | collective-permute-start | bytes 98312 | tf_op jit(solution)/shard_map/ppermute | solution.py:15
  12.9 7.2 %copy-start.4 = (bf16[4,2,4,8,128]{4,3,2,1,0:T(8,128)(2,1)S(1)}, bf16[4,2,4,8,128]{4,3,2,1,0:T(8,128)(2,1)}, u32[]{:S(2)}) copy-start(bf16[4,2,4,8,128]{4,3,2,1,0:T(8,128)(2,1)} %param.6) | copy-start | bytes 196612
  13.0 5.9 %collective-permute-start.1 = (bf16[4,1,4,8,128]{4,3,2,1,0:T(8,128)(2,1)S(1)}, bf16[4,1,4,8,128]{4,3,2,1,0:T(8,128)(2,1)S(1)}, u32[]{:S(2)}, u32[]{:S(2)}) collective-permute-start(bf16[4,1,4,8,128]{4,3,2,1,0:T(8,128)(2,1)S(1)} %get-tuple-element.64), channel_id=1, source_target_pairs={{4,0},{8,4},{12,8},{5,1},{9,5},{13,9},{6,2},{10,6},{14,10},{7,3},{... | collective-permute-start | bytes 98312 | tf_op jit(solution)/shard_map/ppermute | solution.py:17
  19.9 1.0 copy-start.6
  24.8 10.9 %copy-start.1 = (bf16[3,3,3,64,256]{4,3,2,1,0:T(8,128)(2,1)S(1)}, bf16[3,3,3,64,256]{4,3,2,1,0:T(8,128)(2,1)}, u32[]{:S(2)}) copy-start(bf16[3,3,3,64,256]{4,3,2,1,0:T(8,128)(2,1)} %param.9) | copy-start | bytes 2654212
  39.2 13.4 %copy-start.8 = (f32[128,4]{0,1:T(4,128)S(1)}, f32[128,4]{0,1:T(4,128)}, u32[]{:S(2)}) copy-start(f32[128,4]{0,1:T(4,128)} %param.11) | copy-start | bytes 6148
  64.7 12.0 %copy-start.2 = (f32[27,64,256]{2,1,0:T(8,128)}, f32[27,64,256]{2,1,0:T(8,128)S(1)}, u32[]{:S(2)}) copy-start(f32[27,64,256]{2,1,0:T(8,128)S(1)} %fusion) | copy-start | bytes 5308420
  66.1 10.5 %all-to-all-start.1 = ((bf16[1,8,4,512]{3,2,0,1:T(4,128)(2,1)}), bf16[1,8,4,512]{3,2,0,1:T(4,128)(2,1)S(1)}, u32[]{:S(2)}, u32[]{:S(2)}) async-start(bf16[1,8,4,512]{3,2,0,1:T(4,128)(2,1)} %reshape.468), calls=%async_computation.1 | async-start | bytes 65536 | tf_op jit(solution)/shard_map/all_to_all | solution.py:163
  71.0 130.2 %all-reduce.33.cloned.1.call-start = ((), (), s32[]{:S(2)}) async-start(), calls=%async_computation.4 | async-start | bytes 5439488 | tf_op jit(solution)/shard_map/psum | solution.py:173
  82.4 0.9 copy-start.5
  201.2 2.3 %copy-start.3 = (f32[3,3,3,64,256]{4,3,2,1,0:T(8,128)S(1)}, f32[3,3,3,64,256]{4,3,2,1,0:T(8,128)}, u32[]{:S(2)}) copy-start(f32[3,3,3,64,256]{4,3,2,1,0:T(8,128)} %get-tuple-element.74) | copy-start | bytes 5308420
  203.5 1.2 copy-start.7
Sparse Core Ops, SparseCore 0:
  42.0 5.8 reduce-scatter.3
  83.4 117.7 all-reduce.32
where the time goes:
time: 214 us; the launch traced here: 213 us
  waiting for transfers between devices  112 us (52%)
  blocking collectives  33.9 us (16%)
  matrix products  23.2 us (11%)
  between operations  16.7 us (8%)
  local copies, waits for them, and re-layouts  13.5 us (6%)
  starting transfers between devices  11.2 us (5%)
  other arithmetic  2.34 us (1%)
    psum x1, waiting for transfers between devices, body(): lax.psum((grad_front, grad_stride, grad_hidden, grad_output, squared), ('...  96.9 us
    psum x1, blocking collectives, body(): lax.psum((grad_front, grad_stride, grad_hidden, grad_output, squared), ('...  20.3 us
    unnamed x27, local copies, waits for them, and re-layouts  10.4 us
    dot_general x54, matrix products, kernel_grad(): lax.dot_general(flat_tap, flat_grad, (((0,), (0,)), ((), ())), preferred_...  10.2 us
    all_to_all x1, blocking collectives, body(): lax.all_to_all(merged, 'slab', split_axis=0, concat_axis=1, tiled=True)  9.32 us
    dot_general x54, matrix products, conv_apply(): jnp.dot(flat_tap, weight[tap_z, tap_x, tap_y], preferred_element_type=jnp...  7.54 us
    unnamed x3, waiting for transfers between devices  6.09 us
    all_to_all x1, waiting for transfers between devices, body(): lax.all_to_all(grad_act.reshape(1, depth, extent_x, extent_y * inner), 's...  4.94 us
  transfers between devices with their start and end apart: 5, of which 5 were waited for; matrix products, arithmetic and copies ran while one was open for 0% of the time, Pallas kernels for 0%

commit v1 on v0

--- a/solution.py
+++ b/solution.py
@@ -171,7 +171,7 @@
     grad_front_pre = (returned * swish_slope(front_pre)).astype(jnp.bfloat16)
     grad_front = kernel_grad(padded, grad_front_pre, thick, extent_x, extent_y, 1)
     grad_front, grad_stride, grad_hidden, grad_output, squared = lax.psum(
-        (grad_front, grad_stride, grad_hidden, grad_output, squared), ("slab", "batch")
+        lax.psum((grad_front, grad_stride, grad_hidden, grad_output, squared), "batch"), "slab"
     )
     loss = (squared / (slabs * batches * outputs)).reshape(1)
     return (grad_front, grad_stride, grad_hidden, grad_output, loss)

time: 214 us -> 282 us (1.32)
  waiting for transfers between devices: 112 us -> 183 us
    psum x1 -> x2, waiting for transfers between devices: 96.9 us -> 167 us  [the longest x1 91.7 us: body(): lax.psum(lax.psum((grad_front, grad_stride, grad_hidden, grad_output, squ...]
    psum x1 -> x2, blocking collectives: 20.3 us -> 18.3 us  [the longest x1 12.7 us: body(): lax.psum(lax.psum((grad_front, grad_stride, grad_hidden, grad_output, squ...]
    unnamed x3 -> x4, waiting for transfers between devices: 6.09 us -> 6.11 us
  transfers between devices with their start and end apart: 5 -> 6, of which waited for: 5 -> 6; matrix products, arithmetic and copies ran while one was open for 0% -> 0% of each run, Pallas kernels for 0% -> 0%
where the time goes in v1:
time: 282 us; the launch traced here: 281 us
  waiting for transfers between devices  183 us (65%)
  blocking collectives  31.9 us (11%)
  matrix products  23.2 us (8%)
  between operations  16.4 us (6%)
  local copies, waits for them, and re-layouts  13.5 us (5%)
  starting transfers between devices  11.3 us (4%)
    psum x1, waiting for transfers between devices, body(): lax.psum(lax.psum((grad_front, grad_stride, grad_hidden, grad_output, squ...  91.7 us
    psum x1, waiting for transfers between devices, body(): lax.psum((grad_front, grad_stride, grad_hidden, grad_output, squared), 'b...  75.3 us
    psum x1, blocking collectives, body(): lax.psum(lax.psum((grad_front, grad_stride, grad_hidden, grad_output, squ...  12.7 us
    unnamed x27, local copies, waits for them, and re-layouts  10.4 us
    dot_general x54, matrix products, kernel_grad(): lax.dot_general(flat_tap, flat_grad, (((0,), (0,)), ((), ())), preferred_...  10.2 us
    all_to_all x1, blocking collectives, body(): lax.all_to_all(merged, 'slab', split_axis=0, concat_axis=1, tiled=True)  9.32 us
    dot_general x54, matrix products, conv_apply(): jnp.dot(flat_tap, weight[tap_z, tap_x, tap_y], preferred_element_type=jnp...  7.54 us
    unnamed x4, waiting for transfers between devices  6.11 us
  transfers between devices with their start and end apart: 6, of which 6 were waited for; matrix products, arithmetic and copies ran while one was open for 0% of the time, Pallas kernels for 0%

profile of v1, /device:TPU:0, one launch (start us, length us, event | category | flops | bytes accessed | tf_op | source)
XLA Modules:
  0.0 281.1 jit_solution(1153166001701639352)
XLA Ops:
  7.2 0.8 fusion.298
  8.0 4.9 %collective-permute-start = (bf16[4,1,4,8,128]{4,3,2,1,0:T(8,128)(2,1)S(1)}, bf16[4,1,4,8,128]{4,3,2,1,0:T(8,128)(2,1)S(1)}, u32[]{:S(2)}, u32[]{:S(2)}) collective-permute-start(bf16[4,1,4,8,128]{4,3,2,1,0:T(8,128)(2,1)S(1)} %get-tuple-element.68), channel_id=1, source_target_pairs={{0,4},{4,8},{8,12},{1,5},{5,9},{9,13},{2,6},{6,10},{10,14},{3,7},{... | collective-permute-start | bytes 98312 | tf_op jit(solution)/shard_map/ppermute | solution.py:15
  13.0 1.4 collective-permute-start.1
  14.5 4.4 %collective-permute-done.1 = bf16[4,1,4,8,128]{4,3,2,1,0:T(8,128)(2,1)S(1)} collective-permute-done((bf16[4,1,4,8,128]{4,3,2,1,0:T(8,128)(2,1)S(1)}, bf16[4,1,4,8,128]{4,3,2,1,0:T(8,128)(2,1)S(1)}, u32[]{:S(2)}, u32[]{:S(2)}) %collective-permute-start.1) | collective-permute-done | bytes 32800 | tf_op jit(solution)/shard_map/ppermute | solution.py:17
  18.9 1.0 select_maximum_fusion
  19.9 0.2 fusion.294
  20.2 0.6 copy-done.6
  25.4 9.3 %all_to_all.8 = bf16[4,2,4,512]{3,2,1,0:T(4,128)(2,1)S(1)} all-to-all(bf16[4,2,4,512]{3,2,1,0:T(4,128)(2,1)S(1)} %fusion.65), channel_id=1, replica_groups=mesh['groups'=2,'slab'=4,'batch'=2,'chan'=2] {'slab'}, dimensions={0} | all-to-all | bytes 65536 | tf_op jit(solution)/shard_map/all_to_all | solution.py:139
  35.1 0.2 fusion.296
  39.2 0.8 copy.165
  40.0 1.9 reshape.469
  41.9 6.1 %reduce-scatter.4.cloned.1.call-done = f32[128,32]{1,0:T(8,128)} async-done(((f32[256,32]{1,0:T(8,128)}), f32[128,32]{1,0:T(8,128)}) %reduce-scatter.4.cloned.1.call-update) | async-done | bytes 16400
  48.0 1.5 reshape.470
  49.5 0.4 copy.166
  50.1 2.5 psum.77
  52.6 1.4 multiply_reduce_fusion.1
  54.4 1.8 all_gather.3
  65.4 0.7 reshape.468
  66.1 4.8 %all-to-all-start.1 = ((bf16[1,8,4,512]{3,2,0,1:T(4,128)(2,1)}), bf16[1,8,4,512]{3,2,0,1:T(4,128)(2,1)S(1)}, u32[]{:S(2)}, u32[]{:S(2)}) async-start(bf16[1,8,4,512]{3,2,0,1:T(4,128)(2,1)} %reshape.468), calls=%async_computation.1 | async-start | bytes 65536 | tf_op jit(solution)/shard_map/all_to_all | solution.py:163
  71.0 0.7 broadcast_multiply_fusion
  71.7 4.9 %all-to-all-done.1 = bf16[1,8,4,512]{3,2,0,1:T(4,128)(2,1)S(1)} async-done(((bf16[1,8,4,512]{3,2,0,1:T(4,128)(2,1)}), bf16[1,8,4,512]{3,2,0,1:T(4,128)(2,1)S(1)}, u32[]{:S(2)}, u32[]{:S(2)}) %all-to-all-start.1) | async-done | bytes 32800 | tf_op jit(solution)/shard_map/all_to_all | solution.py:163
  76.8 0.2 fusion.54
  77.4 0.2 fusion.51
  77.8 0.2 fusion.50
  78.0 0.2 fusion.49
  78.2 0.2 fusion.48
  78.5 0.2 fusion.47
  78.7 0.2 fusion.46
  78.9 0.2 fusion.45
  79.1 0.2 fusion.44
  79.3 0.2 fusion.43
  79.5 0.2 fusion.42
  79.7 0.2 fusion.41
  79.9 0.2 fusion.40
  80.5 0.2 fusion.37
  81.1 0.2 fusion.34
  81.5 0.2 fusion.33
  81.7 0.2 fusion.32
  81.9 0.2 fusion.31
  82.1 0.2 fusion.30
  82.4 0.9 copy-done.5
  83.3 75.3 %all-reduce.38.cloned.1.call-done = (f32[3,3,3,128,64]{3,4,2,1,0:T(8,128)}, f32[3,3,3,64,256]{4,3,2,1,0:T(8,128)}, f32[128,128]{1,0:T(8,128)}) async-done(((f32[3,3,3,128,64]{3,4,2,1,0:T(8,128)}, f32[3,3,3,64,256]{4,3,2,1,0:T(8,128)}, f32[128,128]{1,0:T(8,128)}), (f32[3,3,3,128,64]{3,4,2,1,0:T(8,128)}, f32[3,3,3,64,256]{4,3,2,1,0:T(8,128)}, f32[128,128]{1,0:T(8,128)})) %all-reduce.38.cloned.1.call-update) | async-done | bytes 2719760 | tf_op jit(solution)/shard_map/psum | solution.py:174
  158.7 5.6 %all-reduce.31 = (f32[128,4]{0,1:T(4,128)S(1)}, f32[]{:T(128)}) all-reduce(f32[128,4]{0,1:T(4,128)S(1)} %broadcast_multiply_fusion.1, f32[]{:T(128)} %get-tuple-element.70), channel_id=1, replica_groups=mesh['groups'=2,'slab'=4,'batch'=2,'chan'=2] {'batch'}, use_global_device_ids=true, to_apply=%region_9.10 | all-reduce | flops 513 | bytes 4104 | tf_op jit(solution)/shard_map/psum | solution.py:174
  164.2 12.7 %all-reduce.29 = (f32[128,4]{0,1:T(4,128)}, f32[]{:T(128)}) all-reduce(f32[128,4]{0,1:T(4,128)S(1)} %get-tuple-element.10, f32[]{:T(128)} %get-tuple-element.11), channel_id=1, replica_groups=mesh['groups'=2,'slab'=4,'batch'=2,'chan'=2] {'slab'}, use_global_device_ids=true, to_apply=%region_10.11 | all-reduce | flops 513 | bytes 4104 | tf_op jit(solution)/shard_map/psum | solution.py:173
  177.6 91.7 %all-reduce.36.cloned.1.call-done = (f32[3,3,3,128,64]{3,4,2,1,0:T(8,128)}, f32[3,3,3,64,256]{4,3,2,1,0:T(8,128)}, f32[128,128]{1,0:T(8,128)}) async-done(((f32[3,3,3,128,64]{3,4,2,1,0:T(8,128)}, f32[3,3,3,64,256]{4,3,2,1,0:T(8,128)}, f32[128,128]{1,0:T(8,128)}), (f32[3,3,3,128,64]{3,4,2,1,0:T(8,128)}, f32[3,3,3,64,256]{4,3,2,1,0:T(8,128)}, f32[128,128]{1,0:T(8,128)})) %all-reduce.36.cloned.1.call-update) | async-done | bytes 2719760 | tf_op jit(solution)/shard_map/psum | solution.py:173
  269.3 2.3 copy.228
  271.6 1.2 copy.229
  272.8 0.6 copy.230
  (208 shorter events, 20.2 us)
Async XLA Ops:
  7.2 42.8 %copy-start = (f32[128,128]{1,0:T(8,128)S(1)}, f32[128,128]{1,0:T(8,128)}, u32[]{:S(2)}) copy-start(f32[128,128]{1,0:T(8,128)} %param.10) | copy-start | bytes 196612
  7.2 40.8 %reduce-scatter.4.cloned.1.call-start = ((), (), s32[]{:S(2)}) async-start(), calls=%async_computation.3 | async-start | bytes 196608
  8.0 6.5 %collective-permute-start = (bf16[4,1,4,8,128]{4,3,2,1,0:T(8,128)(2,1)S(1)}, bf16[4,1,4,8,128]{4,3,2,1,0:T(8,128)(2,1)S(1)}, u32[]{:S(2)}, u32[]{:S(2)}) collective-permute-start(bf16[4,1,4,8,128]{4,3,2,1,0:T(8,128)(2,1)S(1)} %get-tuple-element.68), channel_id=1, source_target_pairs={{0,4},{4,8},{8,12},{1,5},{5,9},{9,13},{2,6},{6,10},{10,14},{3,7},{... | collective-permute-start | bytes 98312 | tf_op jit(solution)/shard_map/ppermute | solution.py:15
  12.9 7.2 %copy-start.4 = (bf16[4,2,4,8,128]{4,3,2,1,0:T(8,128)(2,1)S(1)}, bf16[4,2,4,8,128]{4,3,2,1,0:T(8,128)(2,1)}, u32[]{:S(2)}) copy-start(bf16[4,2,4,8,128]{4,3,2,1,0:T(8,128)(2,1)} %param.6) | copy-start | bytes 196612
  13.0 5.9 %collective-permute-start.1 = (bf16[4,1,4,8,128]{4,3,2,1,0:T(8,128)(2,1)S(1)}, bf16[4,1,4,8,128]{4,3,2,1,0:T(8,128)(2,1)S(1)}, u32[]{:S(2)}, u32[]{:S(2)}) collective-permute-start(bf16[4,1,4,8,128]{4,3,2,1,0:T(8,128)(2,1)S(1)} %get-tuple-element.69), channel_id=1, source_target_pairs={{4,0},{8,4},{12,8},{5,1},{9,5},{13,9},{6,2},{10,6},{14,10},{7,3},{... | collective-permute-start | bytes 98312 | tf_op jit(solution)/shard_map/ppermute | solution.py:17
  19.9 1.0 copy-start.6
  24.8 10.9 %copy-start.1 = (bf16[3,3,3,64,256]{4,3,2,1,0:T(8,128)(2,1)S(1)}, bf16[3,3,3,64,256]{4,3,2,1,0:T(8,128)(2,1)}, u32[]{:S(2)}) copy-start(bf16[3,3,3,64,256]{4,3,2,1,0:T(8,128)(2,1)} %param.9) | copy-start | bytes 2654212
  39.2 13.4 %copy-start.8 = (f32[128,4]{0,1:T(4,128)S(1)}, f32[128,4]{0,1:T(4,128)}, u32[]{:S(2)}) copy-start(f32[128,4]{0,1:T(4,128)} %param.11) | copy-start | bytes 6148
  64.7 12.0 %copy-start.2 = (f32[27,64,256]{2,1,0:T(8,128)}, f32[27,64,256]{2,1,0:T(8,128)S(1)}, u32[]{:S(2)}) copy-start(f32[27,64,256]{2,1,0:T(8,128)S(1)} %fusion) | copy-start | bytes 5308420
  66.1 10.5 %all-to-all-start.1 = ((bf16[1,8,4,512]{3,2,0,1:T(4,128)(2,1)}), bf16[1,8,4,512]{3,2,0,1:T(4,128)(2,1)S(1)}, u32[]{:S(2)}, u32[]{:S(2)}) async-start(bf16[1,8,4,512]{3,2,0,1:T(4,128)(2,1)} %reshape.468), calls=%async_computation.1 | async-start | bytes 65536 | tf_op jit(solution)/shard_map/all_to_all | solution.py:163
  71.0 87.6 %all-reduce.38.cloned.1.call-start = ((), (), s32[]{:S(2)}) async-start(), calls=%async_computation.5 | async-start | bytes 5439488 | tf_op jit(solution)/shard_map/psum | solution.py:174
  82.4 0.9 copy-start.5
  83.3 186.0 %all-reduce.36.cloned.1.call-start = ((), (), s32[]{:S(2)}) async-start(), calls=%async_computation.4 | async-start | bytes 5439488 | tf_op jit(solution)/shard_map/psum | solution.py:173
  269.3 2.3 copy-start.3
  271.6 1.2 copy-start.7
Sparse Core Ops, SparseCore 0:
  42.0 5.8 reduce-scatter.3
  83.4 75.1 all-reduce.37
  161.2 108.0 all-reduce.35
